TPU v7x, 128 devices: a whole 4x4x4 slice. The times are simulated.
128 devices in a mesh: grp: 8 (over z, x_hi), blk: 16 (over x_lo, y, core).
Axes of the slice: x: 4 (x_hi: 2, x_lo: 2; x = x_hi * 2 + x_lo), y: 4, z: 4, core: 2. Of those that a mesh axis runs over, the one named last changes fastest.
Arguments:
- slab: bfloat16 [32, 4096, 4096], P('grp', 'blk'), may hold values from -0.59765625 to 0.59765625
- block_mask: int32 [8, 128, 128], P('grp', 'blk'), may hold values 0 or 1
- orbitals: bfloat16 [4096, 1024], P('blk'), may hold values from -0.09375 to 0.09375
- margin: bfloat16 [4096, 4096], P('blk', 'grp'), as said below
- env_flag: int32 [1024], replicated, may hold values from 0 to 1
Outputs:
- projected: float32 [4096, 4096], P('blk', 'grp')
Inputs may be any that keep to these rules, and one draw needn't show every extreme that they name: margin is symmetric positive definite with unit diagonal.
All inputs are finite; a program needn't handle non-finite values. No bound on the sum of `block_mask` on one device may be relied on, other than what follows from the above.
Results may differ from a plain program's by a relative error of at most 0.003.
Values may be sent and summed in bfloat16 or wider, within the bound.
No kernel may reach another device: no remote copies, remote signals or barrier semaphores. Data moves between devices by JAX's collectives and lax.ppermute only.
A program may use at most 128 MiB of HBM per device.

v0:
```python
import jax
import jax.numpy as jnp
from jax import lax
from jax.sharding import PartitionSpec as P

ATILE = 32


def inner_rows(left, right):
    return lax.dot_general(
        left, right, (((0,), (0,)), ((), ())), preferred_element_type=jnp.float32
    )


def pair_block(half, other):
    return jnp.einsum("pmi,pni->mn", half, other, preferred_element_type=jnp.float32)


def on_device(slab, block_mask, orbitals, margin, env_flag):
    aux_dev, ao_dev, nao = slab.shape
    keep_tile = jnp.repeat(jnp.repeat(block_mask[0], ATILE, axis=0), ATILE, axis=1).astype(
        jnp.bfloat16
    )
    masked = slab * keep_tile[None, :, :]
    whole_c = lax.all_gather(orbitals, "blk", axis=0, tiled=True)
    occ = whole_c.shape[1]
    half = jnp.dot(
        masked.reshape(aux_dev * ao_dev, nao), whole_c, preferred_element_type=jnp.float32
    )
    half = half.astype(jnp.bfloat16).reshape(aux_dev, ao_dev, occ)
    position = lax.axis_index("blk")
    rows_k = pair_block(half, lax.all_gather(half, "blk", axis=1, tiled=True))
    k_tile = lax.psum_scatter(rows_k, "grp", scatter_dimension=1, tiled=True)
    width = k_tile.shape[1]
    ce_whole = whole_c * env_flag.astype(jnp.bfloat16)[None, :]
    ce_rows = lax.dynamic_slice_in_dim(ce_whole, position * ao_dev, ao_dev, 0)
    ce_cols = lax.dynamic_slice_in_dim(ce_whole, lax.axis_index("grp") * width, width, 0)
    k_bf = k_tile.astype(jnp.bfloat16)
    left_part = inner_rows(ce_rows, k_bf)
    envov_part = inner_rows(ce_rows, margin)
    left_env, env_margin = lax.psum((left_part, envov_part), "blk")
    right_part = jnp.dot(k_bf, ce_cols, preferred_element_type=jnp.float32)
    ovenv_part = jnp.dot(margin, ce_cols, preferred_element_type=jnp.float32)
    right_env, margin_env = lax.psum((right_part, ovenv_part), "grp")
    first = jnp.dot(
        margin_env.astype(jnp.bfloat16),
        left_env.astype(jnp.bfloat16),
        preferred_element_type=jnp.float32,
    )
    second = jnp.dot(
        right_env.astype(jnp.bfloat16),
        env_margin.astype(jnp.bfloat16),
        preferred_element_type=jnp.float32,
    )
    return k_tile - first - second


def solution(mesh):
    placed = (P("grp", "blk", None), P("grp", "blk", None), P("blk", None), P("blk", "grp"), P())
    return jax.shard_map(
        on_device, mesh=mesh, in_specs=placed, out_specs=P("blk", "grp"), check_vma=False
    )
```

profile of v0, /device:TPU:0, one launch (start us, length us, event | category | flops | bytes accessed | tf_op | source)
XLA Modules:
  0.0 537.7 jit_solution(16283713551685349303)
XLA Ops:
  6.5 0.0 copy-start
  6.5 0.0 all-gather.3.cloned.1.call-start
  6.5 0.7 all-gather.3.cloned.1.call-update
  7.3 0.0 all-gather.5.cloned.1.call-start
  7.3 0.7 convert_bitcast_fusion
  8.0 0.1 copy.8
  8.1 1.5 broadcast_in_dim.9
  9.6 2.9 copy.9
  12.5 7.5 %broadcast_multiply_fusion.1 = bf16[4,256,4096]{2,1,0:T(8,128)(2,1)} fusion(bf16[4,256,4096]{2,1,0:T(8,128)(2,1)} %param.5, bf16[256,4096]{1,0:T(8,128)(2,1)S(1)} %copy.9), kind=kLoop, calls=%fused_computation.2 | loop fusion | flops 4194304 | bytes 18874368 | tf_op jit(solution)/shard_map/mul | solution.py:24
  20.0 43.7 %all-gather.3.cloned.1.call-done = bf16[4096,1024]{1,0:T(8,128)(2,1)} async-done(((bf16[256,1024]{1,0:T(8,128)(2,1)}), bf16[4096,1024]{1,0:T(8,128)(2,1)}) %all-gather.3.cloned.1.call-update) | async-done | bytes 8388624 | tf_op jit(solution)/shard_map/all_gather | solution.py:25
  63.7 14.7 %convolution_convert_fusion = bf16[1024,1024]{1,0:T(8,128)(2,1)} fusion(bf16[1024,4096]{1,0:T(8,128)(2,1)} %bitcast.20, bf16[4096,1024]{1,0:T(8,128)(2,1)} %all-gather.3.cloned.1.call-done), kind=kOutput, calls=%fused_computation.3 | convolution fusion | flops 8590983168 | bytes 18874368 | tf_op jit(solution)/shard_map/dot_general | solution.py:27
  78.3 0.0 all-gather.5.cloned.1.call-update
  78.4 0.0 copy-start.2
  78.4 0.0 reduce-scatter.2.cloned.1.call-start
  78.4 171.6 %all-gather.5.cloned.1.call-done = bf16[4,4096,1024]{2,1,0:T(8,128)(2,1)} async-done(((bf16[4,256,1024]{2,1,0:T(8,128)(2,1)}), bf16[4,4096,1024]{2,1,0:T(8,128)(2,1)}) %all-gather.5.cloned.1.call-update) | async-done | bytes 33554448 | tf_op jit(solution)/shard_map/all_gather | solution.py:32
  250.1 17.5 %convolution_bitcast_fusion = f32[256,4096]{1,0:T(8,128)} fusion(bf16[4,256,1024]{2,1,0:T(8,128)(2,1)} %bitcast.23, bf16[4,4096,1024]{2,1,0:T(8,128)(2,1)} %all-gather.5.cloned.1.call-done), kind=kOutput, calls=%fused_computation | convolution fusion | flops 8589934592 | bytes 39845888 | tf_op jit(solution)/shard_map/pmi,pni->mn/dot_general | solution.py:16
  267.5 0.0 reduce-scatter.2.cloned.1.call-update
  267.6 0.0 copy-done.2
  267.6 7.2 %broadcast_multiply_fusion = bf16[4096,1024]{1,0:T(8,128)(2,1)} fusion(bf16[4096,1024]{1,0:T(8,128)(2,1)} %all-gather.3.cloned.1.call-done, bf16[1024]{0:T(1024)(128)(2,1)S(1)} %convert_element_type.44), kind=kLoop, calls=%fused_computation.1 | loop fusion | flops 4194304 | bytes 16779264 | tf_op jit(solution)/shard_map/mul | solution.py:35
  274.7 0.0 copy-done
  274.7 1.5 fusion.7
  276.3 2.7 convolution_bitcast_fusion.1
  279.0 74.5 %reduce-scatter.2.cloned.1.call-done = f32[256,512]{1,0:T(8,128)} async-done(((f32[256,4096]{1,0:T(8,128)}), f32[256,512]{1,0:T(8,128)}) %reduce-scatter.2.cloned.1.call-update) | async-done | bytes 524304 | tf_op jit(solution)/shard_map/reduce_scatter | solution.py:33
  353.4 0.0 copy-start.1
  353.5 3.1 fusion.9
  356.5 2.8 fusion.2
  359.4 71.0 %all-reduce.4 = (bf16[1024,512]{1,0:T(8,128)(2,1)}, bf16[1024,512]{1,0:T(8,128)(2,1)}) all-reduce(f32[1024,512]{1,0:T(8,128)} %fusion.9, f32[1024,512]{1,0:T(8,128)S(1)} %fusion.7), channel_id=1, replica_groups=mesh['grp'=8,'blk'=16] {'blk'}, use_global_device_ids=true, to_apply=%region_2.0 | all-reduce | flops 1048576 | bytes 6291456 | tf_op jit(solution)/shard_map/psum | solution.py:41
  430.4 96.6 %all-reduce.5 = (bf16[256,1024]{0,1:T(8,128)(2,1)S(1)}, bf16[256,1024]{1,0:T(8,128)(2,1)S(1)}) all-reduce(f32[256,1024]{0,1:T(8,128)} %convolution_bitcast_fusion.1, f32[256,1024]{1,0:T(8,128)} %fusion.2), channel_id=1, replica_groups=mesh['grp'=8,'blk'=16] {'grp'}, use_global_device_ids=true, to_apply=%region_1.0 | all-reduce | flops 524288 | bytes 3145728 | tf_op jit(solution)/shard_map/psum | solution.py:44
  527.0 0.0 copy-done.1
  527.0 1.7 convolution_subtract_fusion.1
  528.7 2.5 convolution_subtract_fusion
  (2 shorter events, 0.0 us)
Async XLA Ops:
  6.5 268.2 %copy-start = (bf16[256,512]{1,0:T(8,128)(2,1)S(1)}, bf16[256,512]{1,0:T(8,128)(2,1)}, u32[]{:S(2)}) copy-start(bf16[256,512]{1,0:T(8,128)(2,1)} %param.8) | copy-start | bytes 786436
  6.5 57.1 %all-gather.3.cloned.1.call-start = ((), (), s32[]{:S(2)}) async-start(), calls=%async_computation.1 | async-start | bytes 8912896 | tf_op jit(solution)/shard_map/all_gather | solution.py:25
  7.3 242.8 %all-gather.5.cloned.1.call-start = ((), (), s32[]{:S(2)}) async-start(), calls=%async_computation.2 | async-start | bytes 35651584 | tf_op jit(solution)/shard_map/all_gather | solution.py:32
  78.4 189.2 %copy-start.2 = (s32[1024]{0:T(1024)S(1)}, s32[1024]{0:T(1024)}, u32[]{:S(2)}) copy-start(s32[1024]{0:T(1024)} %param.9) | copy-start | bytes 12292
  78.4 275.1 %reduce-scatter.2.cloned.1.call-start = ((), (), s32[]{:S(2)}) async-start(), calls=%async_computation.3 | async-start | bytes 4718592 | tf_op jit(solution)/shard_map/reduce_scatter | solution.py:33
  353.4 173.6 %copy-start.1 = (f32[256,512]{1,0:T(8,128)S(1)}, f32[256,512]{1,0:T(8,128)}, u32[]{:S(2)}) copy-start(f32[256,512]{1,0:T(8,128)} %reduce-scatter.2.cloned.1.call-done) | copy-start | bytes 1572868
Sparse Core Ops, SparseCore 0:
  9.1 54.5 all-gather.2
  78.5 171.5 all-gather.4
  267.7 85.7 reduce-scatter.1
where the time goes:
time: 538 us
  waiting for transfers between devices  291 us (54%)
  blocking collectives  168 us (31%)
  matrix products  46.4 us (9%)
  other arithmetic  15.3 us (3%)
  between operations  13.2 us (2%)
    all_gather x1, waiting for transfers between devices, on_device(): rows_k = pair_block(half, lax.all_gather(half, 'blk', axis=1, tiled=True))  172 us
    psum x1, blocking collectives, on_device(): right_env, margin_env = lax.psum((right_part, ovenv_part), 'grp')  96.6 us
    reduce_scatter x1, waiting for transfers between devices, on_device(): k_tile = lax.psum_scatter(rows_k, 'grp', scatter_dimension=1, tiled=True)  74.5 us
    psum x1, blocking collectives, on_device(): left_env, env_margin = lax.psum((left_part, envov_part), 'blk')  71 us
    all_gather x1, waiting for transfers between devices, on_device(): whole_c = lax.all_gather(orbitals, 'blk', axis=0, tiled=True)  43.7 us
    dot_general x1, matrix products, pair_block(): jnp.einsum('pmi,pni->mn', half, other, preferred_element_type=jnp.float32)  17.5 us
    dot_general x1, matrix products, on_device(): jnp.dot(masked.reshape(aux_dev * ao_dev, nao), whole_c, preferred_element...  14.7 us
  transfers between devices with their start and end apart: 3, of which 3 were waited for; matrix products, arithmetic and copies ran while one was open for 4% of the time, Pallas kernels for 0%

commit v1 on v0

--- a/solution.py
+++ b/solution.py
@@ -22,7 +22,9 @@
         jnp.bfloat16
     )
     masked = slab * keep_tile[None, :, :]
-    whole_c = lax.all_gather(orbitals, "blk", axis=0, tiled=True)
+    whole_c = jnp.concatenate(
+        lax.all_to_all(jnp.stack([orbitals] * lax.axis_size("blk")), "blk", 0, 0), axis=0
+    )
     occ = whole_c.shape[1]
     half = jnp.dot(
         masked.reshape(aux_dev * ao_dev, nao), whole_c, preferred_element_type=jnp.float32

time: 538 us -> 622 us (1.16)
  waiting for transfers between devices: 291 us -> 363 us
    all_to_all x0 -> x1, waiting for transfers between devices: none -> 111 us  [on_device(): lax.all_to_all(jnp.stack([orbitals] * lax.axis_size('blk')), 'blk', 0, 0)]
    all_gather x1 -> x0, waiting for transfers between devices: 43.7 us -> none  [on_device(): whole_c = lax.all_gather(orbitals, 'blk', axis=0, tiled=True)]
    all_gather x1, waiting for transfers between devices: 172 us -> 178 us  [on_device(): rows_k = pair_block(half, lax.all_gather(half, 'blk', axis=1, tiled=True))]
where the time goes in v1:
time: 622 us; the launch traced here: 621 us
  waiting for transfers between devices  363 us (58%)
  blocking collectives  168 us (27%)
  matrix products  46.4 us (7%)
  other arithmetic  14.6 us (2%)
  between operations  13.5 us (2%)
  local copies, waits for them, and re-layouts  9.95 us (2%)
    all_gather x1, waiting for transfers between devices, on_device(): rows_k = pair_block(half, lax.all_gather(half, 'blk', axis=1, tiled=True))  178 us
    all_to_all x1, waiting for transfers between devices, on_device(): lax.all_to_all(jnp.stack([orbitals] * lax.axis_size('blk')), 'blk', 0, 0)  111 us
    psum x1, blocking collectives, on_device(): right_env, margin_env = lax.psum((right_part, ovenv_part), 'grp')  96.7 us
    reduce_scatter x1, waiting for transfers between devices, on_device(): k_tile = lax.psum_scatter(rows_k, 'grp', scatter_dimension=1, tiled=True)  74.5 us
    psum x1, blocking collectives, on_device(): left_env, env_margin = lax.psum((left_part, envov_part), 'blk')  71 us
    dot_general x1, matrix products, pair_block(): jnp.einsum('pmi,pni->mn', half, other, preferred_element_type=jnp.float32)  17.5 us
    dot_general x1, matrix products, on_device(): jnp.dot(masked.reshape(aux_dev * ao_dev, nao), whole_c, preferred_element...  14.7 us
  transfers between devices with their start and end apart: 3, of which 3 were waited for; matrix products, arithmetic and copies ran while one was open for 4% of the time, Pallas kernels for 0%

profile of v1, /device:TPU:0, one launch (start us, length us, event | category | flops | bytes accessed | tf_op | source)
XLA Modules:
  0.0 621.4 jit_solution(15145853452471531590)
XLA Ops:
  6.5 0.0 copy-start
  6.5 5.4 stack.2
  11.9 0.0 copy-start.2
  11.9 5.8 all-to-all-start
  17.7 0.0 all-gather.2.cloned.1.call-start
  17.8 0.0 copy-done.2
  17.8 0.1 copy.8
  17.9 1.5 broadcast_in_dim.9
  19.4 2.9 copy.9
  22.3 7.4 %broadcast_multiply_fusion.1 = bf16[4,256,4096]{2,1,0:T(8,128)(2,1)} fusion(bf16[4,256,4096]{2,1,0:T(8,128)(2,1)} %param.5, bf16[256,4096]{1,0:T(8,128)(2,1)S(1)} %copy.9), kind=kLoop, calls=%fused_computation.2 | loop fusion | flops 4194304 | bytes 18874368 | tf_op jit(solution)/shard_map/mul | solution.py:24
  29.8 110.9 %all-to-all-done = bf16[16,256,1024]{2,1,0:T(8,128)(2,1)} async-done(((bf16[16,256,1024]{2,1,0:T(8,128)(2,1)}), bf16[16,256,1024]{2,1,0:T(8,128)(2,1)}, u32[]{:S(2)}, u32[]{:S(2)}) %all-to-all-start) | async-done | bytes 8388640 | tf_op jit(solution)/shard_map/all_to_all | solution.py:26
  140.6 14.7 %convolution_convert_fusion = bf16[1024,1024]{1,0:T(8,128)(2,1)} fusion(bf16[1024,4096]{1,0:T(8,128)(2,1)} %bitcast.22, bf16[4096,1024]{1,0:T(8,128)(2,1)} %bitcast.4), kind=kOutput, calls=%fused_computation.3 | convolution fusion | flops 8590983168 | bytes 18874368 | tf_op jit(solution)/shard_map/dot_general | solution.py:29
  155.4 0.0 all-gather.2.cloned.1.call-update
  155.4 0.0 copy-start.3
  155.4 0.0 reduce-scatter.2.cloned.1.call-start
  155.4 178.0 %all-gather.2.cloned.1.call-done = bf16[4,4096,1024]{2,1,0:T(8,128)(2,1)} async-done(((bf16[4,256,1024]{2,1,0:T(8,128)(2,1)}), bf16[4,4096,1024]{2,1,0:T(8,128)(2,1)}) %all-gather.2.cloned.1.call-update) | async-done | bytes 33554448 | tf_op jit(solution)/shard_map/all_gather | solution.py:34
  333.4 17.5 %convolution_bitcast_fusion = f32[256,4096]{1,0:T(8,128)} fusion(bf16[4,256,1024]{2,1,0:T(8,128)(2,1)} %bitcast.25, bf16[4,4096,1024]{2,1,0:T(8,128)(2,1)} %all-gather.2.cloned.1.call-done), kind=kOutput, calls=%fused_computation | convolution fusion | flops 8589934592 | bytes 39845888 | tf_op jit(solution)/shard_map/pmi,pni->mn/dot_general | solution.py:16
  350.9 0.0 reduce-scatter.2.cloned.1.call-update
  350.9 0.0 copy-done.3
  350.9 7.2 %broadcast_multiply_fusion = bf16[4096,1024]{1,0:T(8,128)(2,1)} fusion(bf16[1024]{0:T(1024)(128)(2,1)S(1)} %convert_element_type.44, bf16[16,256,1024]{2,1,0:T(8,128)(2,1)} %all-to-all-done), kind=kLoop, calls=%fused_computation.1 | loop fusion | flops 4194304 | bytes 16779264 | tf_op jit(solution)/shard_map/mul | solution.py:37
  358.1 0.0 copy-done
  358.1 1.5 fusion.7
  359.6 2.7 convolution_bitcast_fusion.1
  362.3 74.5 %reduce-scatter.2.cloned.1.call-done = f32[256,512]{1,0:T(8,128)} async-done(((f32[256,4096]{1,0:T(8,128)}), f32[256,512]{1,0:T(8,128)}) %reduce-scatter.2.cloned.1.call-update) | async-done | bytes 524304 | tf_op jit(solution)/shard_map/reduce_scatter | solution.py:35
  436.8 0.0 copy-start.1
  436.8 3.1 fusion.9
  439.9 2.8 fusion.2
  442.7 71.0 %all-reduce.4 = (bf16[1024,512]{1,0:T(8,128)(2,1)}, bf16[1024,512]{1,0:T(8,128)(2,1)}) all-reduce(f32[1024,512]{1,0:T(8,128)} %fusion.9, f32[1024,512]{1,0:T(8,128)S(1)} %fusion.7), channel_id=1, replica_groups=mesh['grp'=8,'blk'=16] {'blk'}, use_global_device_ids=true, to_apply=%region_2.0 | all-reduce | flops 1048576 | bytes 6291456 | tf_op jit(solution)/shard_map/psum | solution.py:43
  513.7 96.7 %all-reduce.5 = (bf16[256,1024]{0,1:T(8,128)(2,1)S(1)}, bf16[256,1024]{1,0:T(8,128)(2,1)S(1)}) all-reduce(f32[256,1024]{0,1:T(8,128)} %convolution_bitcast_fusion.1, f32[256,1024]{1,0:T(8,128)} %fusion.2), channel_id=1, replica_groups=mesh['grp'=8,'blk'=16] {'grp'}, use_global_device_ids=true, to_apply=%region_1.0 | all-reduce | flops 524288 | bytes 3145728 | tf_op jit(solution)/shard_map/psum | solution.py:46
  610.4 0.0 copy-done.1
  610.4 1.7 convolution_subtract_fusion.1
  612.1 2.5 convolution_subtract_fusion
  (3 shorter events, 0.0 us)
Async XLA Ops:
  6.5 351.6 %copy-start = (bf16[256,512]{1,0:T(8,128)(2,1)S(1)}, bf16[256,512]{1,0:T(8,128)(2,1)}, u32[]{:S(2)}) copy-start(bf16[256,512]{1,0:T(8,128)(2,1)} %param.8) | copy-start | bytes 786436
  11.9 5.8 copy-start.2
  11.9 128.7 %all-to-all-start = ((bf16[16,256,1024]{2,1,0:T(8,128)(2,1)}), bf16[16,256,1024]{2,1,0:T(8,128)(2,1)}, u32[]{:S(2)}, u32[]{:S(2)}) async-start(bf16[16,256,1024]{2,1,0:T(8,128)(2,1)} %stack.2), calls=%async_computation | async-start | bytes 16777216 | tf_op jit(solution)/shard_map/all_to_all | solution.py:26
  17.7 315.7 %all-gather.2.cloned.1.call-start = ((), (), s32[]{:S(2)}) async-start(), calls=%async_computation.2 | async-start | bytes 35651584 | tf_op jit(solution)/shard_map/all_gather | solution.py:34
  155.4 195.5 %copy-start.3 = (s32[1024]{0:T(1024)S(1)}, s32[1024]{0:T(1024)}, u32[]{:S(2)}) copy-start(s32[1024]{0:T(1024)} %param.9) | copy-start | bytes 12292
  155.4 281.4 %reduce-scatter.2.cloned.1.call-start = ((), (), s32[]{:S(2)}) async-start(), calls=%async_computation.3 | async-start | bytes 4718592 | tf_op jit(solution)/shard_map/reduce_scatter | solution.py:35
  436.8 173.6 %copy-start.1 = (f32[256,512]{1,0:T(8,128)S(1)}, f32[256,512]{1,0:T(8,128)}, u32[]{:S(2)}) copy-start(f32[256,512]{1,0:T(8,128)} %reduce-scatter.2.cloned.1.call-done) | copy-start | bytes 1572868
Sparse Core Ops, SparseCore 0:
  155.5 177.8 all-gather.1
  351.0 85.6 reduce-scatter.1
